TPU v7x, 128 devices: a whole 4x4x4 slice. The times are simulated.
128 devices in a mesh: tm: 8 (over x, core), ctx: 16 (over y, z).
Axes of the slice: x: 4, y: 4, z: 4, core: 2. Of those that a mesh axis runs over, the one named last changes fastest.
Arguments:
- iterate: float32 [8, 2688, 1536], P('tm', 'ctx'), may hold values from -6 to 6
- anchor: float32 [2688, 1536], P('ctx'), may hold values from -6 to 6
- frame_index: int32 [2688], P('ctx'), may hold values from 0 to 15, never falling along the last dimension, each value on 1 to 336 neighbouring positions
- noise_steps: int32 [8, 16], P('tm'), may hold values from 0 to 11
- qkv_weight: bfloat16 [1536, 4608], replicated, may hold values from -0.15625 to 0.15625
- out_weight: bfloat16 [1536, 1536], replicated, may hold values from -0.15625 to 0.15625
- mod_weight: bfloat16 [256, 4608], replicated, may hold values from -0.375 to 0.375
Outputs:
- updated: float32 [8, 2688, 1536], P('tm', 'ctx')
Inputs may be any that keep to these rules, and one draw needn't show every extreme that they name: `frame_index`: frame numbers never fall along the sequence; each of the 16 frames holds 1 to 336 tokens.
All inputs are finite; a program needn't handle non-finite values.
Results may differ from a plain program's by a relative error of at most 0.00051.
Values may be sent and summed in bfloat16 or wider, within the bound.
No kernel may reach another device: no remote copies, remote signals or barrier semaphores. Data moves between devices by JAX's collectives and lax.ppermute only.
A program may use at most 192 MiB of HBM per device.

v0:
```python
import math
import jax
import jax.numpy as jnp
from jax import lax
from jax.sharding import PartitionSpec as P

HD = 128
NSCHED = 12
shift_factor = 5.0
norm_eps = 1e-06


def carried_in(part, axis, combine, identity):
    place = lax.axis_index(axis)
    gathered = lax.all_gather(part, axis)
    state = jnp.zeros_like(part) + jnp.asarray(identity, part.dtype)

    def one(turn, state):
        return combine(state, lax.dynamic_index_in_dim(gathered, turn, 0, False))

    return lax.fori_loop(0, place, one, state)


def noise_level(level_index):
    fraction = level_index / NSCHED
    return shift_factor * fraction / (1.0 + (shift_factor - 1.0) * fraction)


def frame_terms(steps_row, mod_weight):
    level_float = steps_row.astype(jnp.float32)
    upper = noise_level(level_float + 1.0)
    lower = noise_level(level_float)
    step_size = upper - lower
    half_freq = mod_weight.shape[0] // 2
    rates = jnp.exp(-math.log(10000.0) * jnp.arange(half_freq, dtype=jnp.float32) / half_freq)
    angles = (1000.0 * upper)[:, None] * rates[None, :]
    features = jnp.concatenate([jnp.cos(angles), jnp.sin(angles)], axis=1).astype(jnp.bfloat16)
    modulation = jnp.dot(features, mod_weight, preferred_element_type=jnp.float32)
    return (modulation, step_size)


def layer_norm(latent):
    center = latent - jnp.mean(latent, axis=-1, keepdims=True)
    spread = jnp.mean(center * center, axis=-1, keepdims=True)
    return center * lax.rsqrt(spread + norm_eps)


def head_norm(projected):
    tok_rows = projected.shape[0]
    model_width = projected.shape[1]
    split = projected.reshape(tok_rows, model_width // HD, HD)
    scaled = split * lax.rsqrt(jnp.mean(split * split, axis=-1, keepdims=True) + norm_eps)
    return scaled.reshape(tok_rows, model_width).astype(jnp.bfloat16)


def attend(query_heads, key_rows, value_rows, frame_piece, frame_index):
    piece_rows = key_rows.shape[0]
    head_count = query_heads.shape[1]
    key_heads = key_rows.reshape(piece_rows, head_count, HD)
    value_heads = value_rows.reshape(piece_rows, head_count, HD)
    scores = jnp.einsum(
        "qhd,khd->hqk", query_heads, key_heads, preferred_element_type=jnp.float32
    ) * HD ** (-0.5)
    allowed = frame_piece[None, :] <= frame_index[:, None]
    weights = jnp.where(allowed[None, :, :], jnp.exp(scores), 0.0)
    numerator = jnp.einsum(
        "hqk,khd->hqd",
        weights.astype(jnp.bfloat16),
        value_heads,
        preferred_element_type=jnp.float32,
    )
    denominator = jnp.sum(weights, axis=-1)
    return (numerator, denominator)


def velocity_drift(latent, steps_row, frame_index, qkv_weight, out_weight, mod_weight):
    tok_rows = latent.shape[0]
    model_width = latent.shape[1]
    head_count = model_width // HD
    frame_count = steps_row.shape[0]
    modulation, step_size = frame_terms(steps_row, mod_weight)
    one_hot = (frame_index[:, None] == jnp.arange(frame_count, dtype=jnp.int32)[None, :]).astype(
        jnp.float32
    )
    tok_mod = jnp.dot(one_hot, modulation, precision=lax.Precision.HIGHEST)
    tok_step = jnp.dot(one_hot, step_size[:, None], precision=lax.Precision.HIGHEST)[:, 0]
    shift_part = tok_mod[:, :model_width]
    scale_part = tok_mod[:, model_width : 2 * model_width]
    gate_part = tok_mod[:, 2 * model_width :]
    normed = (layer_norm(latent) * (1.0 + scale_part) + shift_part).astype(jnp.bfloat16)
    projected = jnp.dot(normed, qkv_weight, preferred_element_type=jnp.float32)
    queries = head_norm(projected[:, :model_width])
    key_rows = head_norm(projected[:, model_width : 2 * model_width])
    values = projected[:, 2 * model_width :].astype(jnp.bfloat16)
    query_heads = queries.reshape(tok_rows, head_count, HD)
    numerator, denominator = attend(
        query_heads,
        lax.all_gather(key_rows, "ctx", axis=0, tiled=True),
        lax.all_gather(values, "ctx", axis=0, tiled=True),
        lax.all_gather(frame_index, "ctx", axis=0, tiled=True),
        frame_index,
    )
    attended = (numerator / denominator[:, :, None]).astype(jnp.bfloat16)
    attended = attended.transpose(1, 0, 2).reshape(tok_rows, model_width)
    branch = jnp.dot(attended, out_weight, preferred_element_type=jnp.float32)
    return -tok_step[:, None] * (latent + gate_part * branch)


def add_terms(earlier, later):
    return earlier + later


def per_device(iterate, anchor, frame_index, noise_steps, qkv_weight, out_weight, mod_weight):
    position = 0
    drifts = [
        velocity_drift(
            iterate[position],
            noise_steps[position],
            frame_index,
            qkv_weight,
            out_weight,
            mod_weight,
        )
    ]
    block_total = drifts[0]
    earlier = carried_in(block_total, "tm", add_terms, jnp.zeros_like(block_total))
    running = earlier
    position = 0
    running = running + drifts[position]
    results = [anchor + running]
    return jnp.stack(results, axis=0)


def solution(mesh):
    placed = (P("tm", "ctx", None), P("ctx", None), P("ctx"), P("tm", None), P(), P(), P())
    return jax.shard_map(
        per_device, mesh=mesh, in_specs=placed, out_specs=P("tm", "ctx", None), check_vma=False
    )
```

profile of v0, /device:TPU:15, one launch (start us, length us, event | category | flops | bytes accessed | tf_op | source)
XLA Modules:
  0.0 275.0 jit_solution(8744244046365026407)
XLA Ops:
  6.6 0.8 multiply_bitcast_fusion
  7.4 1.6 reduce_sum.45
  8.9 1.5 multiply_reduce_fusion
  10.4 0.1 fusion.36
  10.5 0.4 fusion.38
  11.0 2.1 fusion.32
  13.1 8.9 %fusion.21 = f32[168,4608]{1,0:T(8,128)S(1)} fusion(bf16[1536,4608]{1,0:T(8,128)(2,1)} %param.13, f32[168,4608]{1,0:T(8,128)S(1)} %fusion.32, f32[1,168,1536]{2,1,0:T(8,128)S(1)} %copy-done.2, f32[168]{0:T(256)S(1)} %add_rsqrt_fusion.2, f32[168]{0:T(256)S(1)} %broadcast_multiply_fusion), kind=kOutput, calls=%fused_computation.29 | convolution fusion | flops 2379718656 | bytes 20350976 | tf_op jit(solution)/shard_map/dot_general | solution.py:91
  22.0 1.7 copy-done.3
  23.8 1.4 slice_multiply_fusion.1
  25.2 1.4 mul.143
  26.7 0.4 reduce_sum.47
  27.1 0.1 copy.25
  27.2 0.1 copy.26
  27.3 1.4 mul.148
  28.8 0.4 reduce_sum.48
  29.2 0.1 copy.27
  29.3 0.1 copy.28
  29.4 0.4 mul.144
  29.8 0.4 mul.149
  30.2 3.2 %fusion.23 = (bf16[21,12,8,128]{3,2,1,0:T(8,128)(2,1)S(1)}, bf16[168,1536]{1,0:T(8,128)(2,1)}) fusion(f32[21,8,12,128]{3,2,1,0:T(8,128)S(1)} %bitcast.64, f32[168,4608]{1,0:T(8,128)} %copy-done.3, f32[21,8,12,128]{3,2,1,0:T(8,128)S(1)} %bitcast.65), kind=kLoop, calls=%fused_computation.30 | loop fusion | flops 1032192 | bytes 5160960
  33.5 0.0 all-gather.7.cloned.1.call-start
  33.6 2.1 slice.49
  35.6 0.0 all-gather.7.cloned.1.call-update
  35.6 0.0 all-gather.9.cloned.1.call-start
  35.7 0.2 fusion.33
  35.9 0.0 copy-done.7
  36.0 0.7 dynamic-slice
  37.3 0.3 dynamic-update-slice
  37.6 59.2 %all-reduce = s32[2688]{0:T(1024)S(1)} all-reduce(s32[2688]{0:T(1024)S(1)} %dynamic-update-slice), channel_id=1, replica_groups=mesh['tm'=8,'ctx'=16] {'ctx'}, use_global_device_ids=true, to_apply=%add | all-reduce | flops 2688 | bytes 21504
  96.7 0.3 broadcast_compare_fusion
  97.1 9.8 %all-gather.5.cloned.1.call-done = bf16[2688,1536]{1,0:T(8,128)(2,1)} async-done(((bf16[168,1536]{1,0:T(8,128)(2,1)}), bf16[2688,1536]{1,0:T(8,128)(2,1)}) %all-gather.5.cloned.1.call-update) | async-done | bytes 8257552 | tf_op jit(solution)/shard_map/all_gather | solution.py:98
  106.9 11.2 %copy.29 = bf16[2688,1536]{0,1:T(8,128)(2,1)} copy(bf16[2688,1536]{1,0:T(8,128)(2,1)} %all-gather.5.cloned.1.call-done) | data formatting | bytes 16515072 | tf_op jit(solution)/shard_map/all_gather | solution.py:98
  118.1 12.6 %fusion = (f32[12,168]{1,0:T(8,128)S(1)}, f32[12,168,2688]{2,1,0:T(8,128)}) fusion(pred[168,2688]{1,0:T(8,128)(4,1)S(1)} %broadcast_compare_fusion, bf16[2688,12,128]{0,2,1:T(8,128)(2,1)} %bitcast.62, bf16[21,12,8,128]{3,2,1,0:T(8,128)(2,1)S(1)} %get-tuple-element.39), kind=kOutput, calls=%fused_computation.2 | convolution fusion | flops 1403521024 | bytes 30909312 | tf_op jit(solution)/shard_map/qhd,khd->hqk/dot_general | solution.py:61
  130.7 48.2 %all-gather.7.cloned.1.call-done = bf16[2688,1536]{1,0:T(8,128)(2,1)} async-done(((bf16[168,1536]{1,0:T(8,128)(2,1)}), bf16[2688,1536]{1,0:T(8,128)(2,1)}) %all-gather.7.cloned.1.call-update) | async-done | bytes 8257552 | tf_op jit(solution)/shard_map/all_gather | solution.py:99
  178.9 11.2 %copy.32 = bf16[2688,1536]{0,1:T(8,128)(2,1)} copy(bf16[2688,1536]{1,0:T(8,128)(2,1)} %all-gather.7.cloned.1.call-done) | data formatting | bytes 16515072 | tf_op jit(solution)/shard_map/all_gather | solution.py:99
  190.1 12.5 %fusion.18 = bf16[12,21,8,128]{3,2,1,0:T(8,128)(2,1)S(1)} fusion(bf16[2688,12,128]{0,2,1:T(8,128)(2,1)} %bitcast.63, f32[12,168,2688]{2,1,0:T(8,128)} %get-tuple-element.46, pred[168,2688]{1,0:T(8,128)(4,1)S(1)} %broadcast_compare_fusion, f32[168,12]{0,1:T(8,128)S(1)} %bitcast.68), kind=kOutput, calls=%fused_computation.27 | convolution fusion | flops 1404039168 | bytes 30909312 | tf_op jit(solution)/shard_map/hqk,khd->hqd/dot_general | solution.py:66
  202.6 4.6 %fusion.8 = f32[168,1536]{1,0:T(8,128)} fusion(bf16[1536,1536]{1,0:T(8,128)(2,1)} %param.14, f32[168,4608]{1,0:T(8,128)} %copy-done.4, f32[1,168,1536]{2,1,0:T(8,128)S(1)} %copy-done.2, bf16[12,21,8,128]{3,2,1,0:T(8,128)(2,1)S(1)} %fusion.18, f32[168]{0:T(256)S(1)} %neg.4), kind=kOutput, calls=%fused_computation.10 | convolution fusion | flops 793497600 | bytes 8331936 | tf_op jit(solution)/shard_map/dot_general | solution.py:105
  207.3 47.7 %all-gather.9.cloned.1.call-done = f32[1344,1536]{1,0:T(8,128)} async-done(((f32[168,1536]{1,0:T(8,128)}), f32[1344,1536]{1,0:T(8,128)}) %all-gather.9.cloned.1.call-update) | async-done | bytes 8257552 | tf_op jit(solution)/shard_map/all_gather | solution.py:15
  254.9 0.1 broadcast_in_dim.10
  255.0 10.8 %while.10 = (s32[]{:T(128)}, f32[168,1536]{1,0:T(8,128)S(1)}, s32[]{:T(128)}, f32[8,168,1536]{2,1,0:T(8,128)}, s32[]{:T(128)}, /*index=5*/s32[]{:T(128)}, s32[]{:T(128)}) while((s32[]{:T(128)}, f32[168,1536]{1,0:T(8,128)S(1)}, s32[]{:T(128)}, f32[8,168,1536]{2,1,0:T(8,128)}, s32[]{:T(128)}, /*index=5*/s32[]{:T(128)}, s32[]{:T(128)}) %tuple.32), condition=%wide.region_6.7_spmd, body=%wide.region_5.6_spmd.sunk | while | flops 258053 | bytes 3096691 | solution.py:21
  255.1 1.6 bitcast_add_fusion.2
  256.7 1.5 bitcast_add_fusion.2
  258.2 1.5 bitcast_add_fusion.2
  259.8 1.5 bitcast_add_fusion.2
  261.3 1.5 bitcast_add_fusion.2
  262.8 1.5 bitcast_add_fusion.2
  264.3 1.5 bitcast_add_fusion.2
  265.8 2.7 add_bitcast_fusion
  (24 shorter events, 0.1 us)
Async XLA Ops:
  6.5 4.0 %copy-start = (bf16[256,4608]{1,0:T(8,128)(2,1)S(1)}, bf16[256,4608]{1,0:T(8,128)(2,1)}, u32[]{:S(2)}) copy-start(bf16[256,4608]{1,0:T(8,128)(2,1)} %param.15) | copy-start | bytes 7077892
  6.5 6.5 %copy-start.2 = (f32[1,168,1536]{2,1,0:T(8,128)S(1)}, f32[1,168,1536]{2,1,0:T(8,128)}, u32[]{:S(2)}) copy-start(f32[1,168,1536]{2,1,0:T(8,128)} %param.9) | copy-start | bytes 3096580
  6.5 100.4 %all-gather.5.cloned.1.call-start = ((), (), s32[]{:S(2)}) async-start(), calls=%async_computation | async-start | bytes 8773632 | tf_op jit(solution)/shard_map/all_gather | solution.py:98
  13.1 8.9 %copy-start.4 = (f32[168,4608]{1,0:T(8,128)}, f32[168,4608]{1,0:T(8,128)S(1)}, u32[]{:S(2)}) copy-start(f32[168,4608]{1,0:T(8,128)S(1)} %fusion.32) | copy-start | bytes 9289732
  22.0 1.8 copy-start.3
  26.6 9.1 %copy-start.5 = (s32[168]{0:T(256)S(1)}, s32[168]{0:T(256)}, u32[]{:S(2)}) copy-start(s32[168]{0:T(256)} %param.11) | copy-start | bytes 2020
  26.6 9.1 %copy-start.6 = (s32[1,16]{1,0:T(1,128)S(1)}, s32[1,16]{1,0:T(1,128)}, u32[]{:S(2)}) copy-start(s32[1,16]{1,0:T(1,128)} %param.12) | copy-start | bytes 196
  26.7 9.3 %copy-start.7 = (u32[128]{0:T(128)S(1)}, u32[128]{0:T(128)}, u32[]{:S(2)}) copy-start(u32[128]{0:T(128)} %constant.59) | copy-start | bytes 1540
  33.5 145.4 %all-gather.7.cloned.1.call-start = ((), (), s32[]{:S(2)}) async-start(), calls=%async_computation.1 | async-start | bytes 8773632 | tf_op jit(solution)/shard_map/all_gather | solution.py:99
  35.6 219.3 %all-gather.9.cloned.1.call-start = ((), (), s32[]{:S(2)}) async-start(), calls=%async_computation.2 | async-start | bytes 9289728 | tf_op jit(solution)/shard_map/all_gather | solution.py:15
  255.0 13.5 %copy-start.1 = (bf16[256,4608]{1,0:T(8,128)(2,1)S(1)}, bf16[256,4608]{1,0:T(8,128)(2,1)}, u32[]{:S(2)}) copy-start(bf16[256,4608]{1,0:T(8,128)(2,1)} %param.15) | copy-start | bytes 7077892
Sparse Core Ops, SparseCore 0:
  33.6 73.2 all-gather.4
  109.1 69.7 all-gather.6
  207.4 47.4 all-gather.8
where the time goes:
time: 276 us; the launch traced here: 275 us
  waiting for transfers between devices  106 us (38%)
  blocking collectives  59.2 us (21%)
  matrix products  41.3 us (15%)
  local copies, waits for them, and re-layouts  31.3 us (11%)
  other arithmetic  23.1 us (8%)
  between operations  14 us (5%)
    unnamed x1, blocking collectives  59.2 us
    all_gather x1, waiting for transfers between devices, velocity_drift(): lax.all_gather(values, 'ctx', axis=0, tiled=True)  48.2 us
    all_gather x1, waiting for transfers between devices, carried_in(): gathered = lax.all_gather(part, axis)  47.7 us
    dot_general x1, matrix products, attend(): jnp.einsum('qhd,khd->hqk', query_heads, key_heads, preferred_element_type...  12.6 us
    dot_general x1, matrix products, attend(): jnp.einsum('hqk,khd->hqd', weights.astype(jnp.bfloat16), value_heads, pre...  12.5 us
    all_gather x1, local copies, waits for them, and re-layouts, velocity_drift(): lax.all_gather(key_rows, 'ctx', axis=0, tiled=True)  11.2 us
    all_gather x1, local copies, waits for them, and re-layouts, velocity_drift(): lax.all_gather(values, 'ctx', axis=0, tiled=True)  11.2 us
    add x7, other arithmetic, add_terms(): return earlier + later  10.6 us
  transfers between devices with their start and end apart: 3, of which 3 were waited for; matrix products, arithmetic and copies ran while one was open for 10% of the time, Pallas kernels for 0%

commit v1 on v0

--- a/solution.py
+++ b/solution.py
@@ -95,7 +95,9 @@
     query_heads = queries.reshape(tok_rows, head_count, HD)
     numerator, denominator = attend(
         query_heads,
-        lax.all_gather(key_rows, "ctx", axis=0, tiled=True),
+        jnp.concatenate(
+            lax.all_to_all(jnp.stack([key_rows] * lax.axis_size("ctx")), "ctx", 0, 0), axis=0
+        ),
         lax.all_gather(values, "ctx", axis=0, tiled=True),
         lax.all_gather(frame_index, "ctx", axis=0, tiled=True),
         frame_index,

time: 276 us -> 390 us (1.41)
  blocking collectives: 59.2 us -> 192 us
  waiting for transfers between devices: 106 us -> 65.7 us
  starting transfers between devices: 0.09 us -> 8.02 us
  local copies, waits for them, and re-layouts: 31.3 us -> 38.7 us
  matrix products: 41.3 us -> 45.2 us
    unnamed x1, blocking collectives: 59.2 us -> 192 us
    all_gather x1, waiting for transfers between devices: 48.2 us -> 0.01 us  [velocity_drift(): lax.all_gather(values, 'ctx', axis=0, tiled=True)]
    another operation x0 -> x2, local copies, waits for them, and re-layouts: none -> 19.4 us  [the longest x1 15.7 us: attend(): key_heads = key_rows.reshape(piece_rows, head_count, HD)]
    all_gather x1, waiting for transfers between devices: 47.7 us -> 65.6 us  [carried_in(): gathered = lax.all_gather(part, axis)]
    all_gather x1 -> x0, local copies, waits for them, and re-layouts: 11.2 us -> none  [velocity_drift(): lax.all_gather(key_rows, 'ctx', axis=0, tiled=True)]
    all_gather x1 -> x0, waiting for transfers between devices: 9.84 us -> none  [velocity_drift(): lax.all_gather(key_rows, 'ctx', axis=0, tiled=True)]
    all_to_all x0 -> x1, starting transfers between devices: none -> 7.98 us  [velocity_drift(): lax.all_to_all(jnp.stack([key_rows] * lax.axis_size('ctx')), 'ctx', 0, 0)]
  transfers between devices with their start and end apart: 3 -> 3, of which waited for: 3 -> 1; matrix products, arithmetic and copies ran while one was open for 10% -> 12% of each run, Pallas kernels for 0% -> 0%
where the time goes in v1:
time: 390 us; the launch traced here: 388 us
  blocking collectives  192 us (49%)
  waiting for transfers between devices  65.7 us (17%)
  matrix products  45.2 us (12%)
  local copies, waits for them, and re-layouts  38.7 us (10%)
  other arithmetic  24.7 us (6%)
  between operations  14.3 us (4%)
  starting transfers between devices  8.02 us (2%)
    unnamed x1, blocking collectives  192 us
    all_gather x1, waiting for transfers between devices, carried_in(): gathered = lax.all_gather(part, axis)  65.6 us
    dot_general x1, matrix products, attend(): jnp.einsum('qhd,khd->hqk', query_heads, key_heads, preferred_element_type...  16.5 us
    another operation x1, local copies, waits for them, and re-layouts, attend(): key_heads = key_rows.reshape(piece_rows, head_count, HD)  15.7 us
    dot_general x1, matrix products, attend(): jnp.einsum('hqk,khd->hqd', weights.astype(jnp.bfloat16), value_heads, pre...  12.5 us
    all_gather x1, local copies, waits for them, and re-layouts, velocity_drift(): lax.all_gather(values, 'ctx', axis=0, tiled=True)  11.7 us
    add x7, other arithmetic, add_terms(): return earlier + later  10.6 us
    dot_general x1, matrix products, velocity_drift(): projected = jnp.dot(normed, qkv_weight, preferred_element_type=jnp.float32)  8.91 us
  transfers between devices with their start and end apart: 3, of which 1 were waited for; matrix products, arithmetic and copies ran while one was open for 12% of the time, Pallas kernels for 0%

profile of v1, /device:TPU:15, one launch (start us, length us, event | category | flops | bytes accessed | tf_op | source)
XLA Modules:
  0.0 388.4 jit_solution(12093800887892175069)
XLA Ops:
  6.6 0.8 multiply_bitcast_fusion
  7.4 1.6 reduce_sum.45
  8.9 1.5 multiply_reduce_fusion
  10.4 0.1 fusion.37
  10.5 0.4 fusion.39
  11.0 2.1 fusion.33
  13.1 8.9 %fusion.23 = f32[168,4608]{1,0:T(8,128)S(1)} fusion(bf16[1536,4608]{1,0:T(8,128)(2,1)} %param.13, f32[168,4608]{1,0:T(8,128)S(1)} %fusion.33, f32[1,168,1536]{2,1,0:T(8,128)S(1)} %copy-done.2, f32[168]{0:T(256)S(1)} %add_rsqrt_fusion.2, f32[168]{0:T(256)S(1)} %broadcast_multiply_fusion), kind=kOutput, calls=%fused_computation.31 | convolution fusion | flops 2379718656 | bytes 20350976 | tf_op jit(solution)/shard_map/dot_general | solution.py:91
  22.0 1.6 copy-done.3
  23.6 0.8 slice.49
  24.5 0.0 all-gather.4.cloned.1.call-update
  24.5 3.0 slice_multiply_fusion.1
  27.5 1.4 mul.143
  28.9 0.4 reduce_sum.47
  29.4 0.1 copy.22
  29.5 0.1 copy.23
  29.6 1.4 mul.148
  31.0 0.4 reduce_sum.48
  31.4 0.1 copy.24
  31.5 0.1 copy.25
  31.7 0.4 mul.144
  32.1 0.4 mul.149
  32.5 3.2 fusion.25
  35.7 3.7 stack.4
  39.5 8.0 %all-to-all-start = ((bf16[16,168,1536]{2,1,0:T(8,128)(2,1)}), bf16[16,168,1536]{2,1,0:T(8,128)(2,1)}, u32[]{:S(2)}, u32[]{:S(2)}) async-start(bf16[16,168,1536]{2,1,0:T(8,128)(2,1)} %stack.4), calls=%async_computation | async-start | bytes 16515072 | tf_op jit(solution)/shard_map/all_to_all | solution.py:99
  47.4 0.0 all-gather.6.cloned.1.call-start
  47.5 0.2 fusion.34
  47.7 0.0 copy-done.8
  47.8 0.7 dynamic-slice
  49.1 0.3 dynamic-update-slice
  49.4 191.7 %all-reduce = s32[2688]{0:T(1024)S(1)} all-reduce(s32[2688]{0:T(1024)S(1)} %dynamic-update-slice), channel_id=1, replica_groups=mesh['tm'=8,'ctx'=16] {'ctx'}, use_global_device_ids=true, to_apply=%add | all-reduce | flops 2688 | bytes 21504
  241.1 0.3 broadcast_compare_fusion
  241.4 15.7 %reshape_reshape.3 = bf16[2688,12,128]{2,1,0:T(8,128)(2,1)} reshape(bf16[16,168,1536]{2,1,0:T(8,128)(2,1)} %all-to-all-done) | data formatting | bytes 16515072 | tf_op jit(solution)/shard_map/reshape;reshape | solution.py:59
  257.1 16.5 %fusion = (f32[12,168]{1,0:T(8,128)S(1)}, f32[12,168,2688]{2,1,0:T(8,128)}) fusion(pred[168,2688]{1,0:T(8,128)(4,1)S(1)} %broadcast_compare_fusion, bf16[2688,12,128]{2,1,0:T(8,128)(2,1)} %reshape_reshape.3, bf16[21,12,8,128]{3,2,1,0:T(8,128)(2,1)S(1)} %copy-done.5), kind=kOutput, calls=%fused_computation.2 | convolution fusion | flops 1403521024 | bytes 30909312 | tf_op jit(solution)/shard_map/qhd,khd->hqk/dot_general | solution.py:61
  273.5 11.7 %copy.28 = bf16[2688,1536]{0,1:T(8,128)(2,1)} copy(bf16[2688,1536]{1,0:T(8,128)(2,1)} %all-gather.4.cloned.1.call-done) | data formatting | bytes 16515072 | tf_op jit(solution)/shard_map/all_gather | solution.py:101
  285.2 12.5 %fusion.20 = bf16[12,21,8,128]{3,2,1,0:T(8,128)(2,1)S(1)} fusion(bf16[2688,12,128]{0,2,1:T(8,128)(2,1)} %bitcast.60, f32[12,168,2688]{2,1,0:T(8,128)} %get-tuple-element.46, pred[168,2688]{1,0:T(8,128)(4,1)S(1)} %broadcast_compare_fusion, f32[168,12]{0,1:T(8,128)S(1)} %bitcast.65), kind=kOutput, calls=%fused_computation.29 | convolution fusion | flops 1404039168 | bytes 30909312 | tf_op jit(solution)/shard_map/hqk,khd->hqd/dot_general | solution.py:66
  297.7 4.6 %fusion.10 = f32[168,1536]{1,0:T(8,128)} fusion(bf16[1536,1536]{1,0:T(8,128)(2,1)} %param.14, f32[168,4608]{1,0:T(8,128)} %copy-done.4, f32[1,168,1536]{2,1,0:T(8,128)S(1)} %copy-done.2, bf16[12,21,8,128]{3,2,1,0:T(8,128)(2,1)S(1)} %fusion.20, f32[168]{0:T(256)S(1)} %neg.4), kind=kOutput, calls=%fused_computation.12 | convolution fusion | flops 793497600 | bytes 8331936 | tf_op jit(solution)/shard_map/dot_general | solution.py:107
  302.3 0.0 all-gather.6.cloned.1.call-update
  302.3 65.6 %all-gather.6.cloned.1.call-done = f32[1344,1536]{1,0:T(8,128)} async-done(((f32[168,1536]{1,0:T(8,128)}), f32[1344,1536]{1,0:T(8,128)}) %all-gather.6.cloned.1.call-update) | async-done | bytes 8257552 | tf_op jit(solution)/shard_map/all_gather | solution.py:15
  368.0 0.1 broadcast_in_dim.10
  368.1 10.8 %while.10 = (s32[]{:T(128)}, f32[168,1536]{1,0:T(8,128)S(1)}, s32[]{:T(128)}, f32[8,168,1536]{2,1,0:T(8,128)}, s32[]{:T(128)}, /*index=5*/s32[]{:T(128)}, s32[]{:T(128)}) while((s32[]{:T(128)}, f32[168,1536]{1,0:T(8,128)S(1)}, s32[]{:T(128)}, f32[8,168,1536]{2,1,0:T(8,128)}, s32[]{:T(128)}, /*index=5*/s32[]{:T(128)}, s32[]{:T(128)}) %tuple.30), condition=%wide.region_6.7_spmd, body=%wide.region_5.6_spmd.sunk | while | flops 258053 | bytes 3096691 | solution.py:21
  368.1 1.6 bitcast_add_fusion.2
  369.8 1.5 bitcast_add_fusion.2
  371.3 1.5 bitcast_add_fusion.2
  372.8 1.5 bitcast_add_fusion.2
  374.3 1.5 bitcast_add_fusion.2
  375.8 1.5 bitcast_add_fusion.2
  377.3 1.5 bitcast_add_fusion.2
  378.8 2.7 add_bitcast_fusion
  (26 shorter events, 0.1 us)
Async XLA Ops:
  6.5 4.0 %copy-start = (bf16[256,4608]{1,0:T(8,128)(2,1)S(1)}, bf16[256,4608]{1,0:T(8,128)(2,1)}, u32[]{:S(2)}) copy-start(bf16[256,4608]{1,0:T(8,128)(2,1)} %param.15) | copy-start | bytes 7077892
  6.5 6.5 %copy-start.2 = (f32[1,168,1536]{2,1,0:T(8,128)S(1)}, f32[1,168,1536]{2,1,0:T(8,128)}, u32[]{:S(2)}) copy-start(f32[1,168,1536]{2,1,0:T(8,128)} %param.9) | copy-start | bytes 3096580
  6.5 267.0 %all-gather.4.cloned.1.call-start = ((), (), s32[]{:S(2)}) async-start(), calls=%async_computation.1 | async-start | bytes 8773632 | tf_op jit(solution)/shard_map/all_gather | solution.py:101
  13.1 8.9 %copy-start.4 = (f32[168,4608]{1,0:T(8,128)}, f32[168,4608]{1,0:T(8,128)S(1)}, u32[]{:S(2)}) copy-start(f32[168,4608]{1,0:T(8,128)S(1)} %fusion.33) | copy-start | bytes 9289732
  22.0 1.6 copy-start.3
  39.5 8.0 %copy-start.6 = (s32[168]{0:T(256)S(1)}, s32[168]{0:T(256)}, u32[]{:S(2)}) copy-start(s32[168]{0:T(256)} %param.11) | copy-start | bytes 2020
  39.5 8.0 %copy-start.7 = (s32[1,16]{1,0:T(1,128)S(1)}, s32[1,16]{1,0:T(1,128)}, u32[]{:S(2)}) copy-start(s32[1,16]{1,0:T(1,128)} %param.12) | copy-start | bytes 196
  39.5 8.3 %copy-start.8 = (u32[128]{0:T(128)S(1)}, u32[128]{0:T(128)}, u32[]{:S(2)}) copy-start(u32[128]{0:T(128)} %constant.59) | copy-start | bytes 1540
  39.5 201.9 %all-to-all-start = ((bf16[16,168,1536]{2,1,0:T(8,128)(2,1)}), bf16[16,168,1536]{2,1,0:T(8,128)(2,1)}, u32[]{:S(2)}, u32[]{:S(2)}) async-start(bf16[16,168,1536]{2,1,0:T(8,128)(2,1)} %stack.4), calls=%async_computation | async-start | bytes 16515072 | tf_op jit(solution)/shard_map/all_to_all | solution.py:99
  47.4 320.5 %all-gather.6.cloned.1.call-start = ((), (), s32[]{:S(2)}) async-start(), calls=%async_computation.2 | async-start | bytes 9289728 | tf_op jit(solution)/shard_map/all_gather | solution.py:15
  241.4 15.7 %copy-start.5 = (bf16[21,12,8,128]{3,2,1,0:T(8,128)(2,1)S(1)}, bf16[21,12,8,128]{3,2,1,0:T(8,128)(2,1)}, u32[]{:S(2)}) copy-start(bf16[21,12,8,128]{3,2,1,0:T(8,128)(2,1)} %get-tuple-element.39) | copy-start | bytes 1548292
  368.1 13.5 %copy-start.1 = (bf16[256,4608]{1,0:T(8,128)(2,1)S(1)}, bf16[256,4608]{1,0:T(8,128)(2,1)}, u32[]{:S(2)}) copy-start(bf16[256,4608]{1,0:T(8,128)(2,1)} %param.15) | copy-start | bytes 7077892
Sparse Core Ops, SparseCore 0:
  24.6 164.9 all-gather.3
  302.5 65.4 all-gather.5
